TPU v7x, 32 devices: a whole 2x2x4 slice. The times are simulated.
32 devices in a mesh: shard: 4 (over y, x), ctx: 2 (over core), tp: 4 (over z).
Axes of the slice: x: 2, y: 2, z: 4, core: 2. Of those that a mesh axis runs over, the one named last changes fastest.
Arguments:
- tokens: bfloat16 [8192, 1024], P(('shard', 'ctx')), may hold values from -6 to 6
- segment_ids: int32 [4, 2048], P('shard'), may hold values from 0 to 3, never falling along the last dimension, each value on 1 to 1024 neighbouring positions
- cotangent: bfloat16 [8192, 1024], P(('shard', 'ctx')), may hold values from -6 to 6
- mixer_gain: float32 [1024], replicated, may hold values from 0.5 to 1.5
- query_weight: bfloat16 [1024, 1024], P('shard', 'tp'), may hold values from -0.1875 to 0.1875
- key_weight: bfloat16 [1024, 1024], P('shard', 'tp'), may hold values from -0.1875 to 0.1875
- value_weight: bfloat16 [1024, 2048], P('shard', 'tp'), may hold values from -0.1875 to 0.1875
- gate_weight: bfloat16 [1024, 2048], P('shard', 'tp'), may hold values from -0.1875 to 0.1875
- decay_weight: bfloat16 [1024, 8], P('shard', 'tp'), may hold values from -0.1875 to 0.1875
- beta_weight: bfloat16 [1024, 8], P('shard', 'tp'), may hold values from -0.1875 to 0.1875
- query_conv: float32 [4, 1024], P(None, 'tp'), may hold values from -2 to 2
- key_conv: float32 [4, 1024], P(None, 'tp'), may hold values from -2 to 2
- value_conv: float32 [4, 2048], P(None, 'tp'), may hold values from -2 to 2
- decay_log: float32 [8], P('tp'), may hold values from -7.6 to -2.3
- decay_bias: float32 [8], P('tp'), may hold values from -3 to 3
- out_gain: float32 [256], replicated, may hold values from 0.5 to 1.5
- output_weight: bfloat16 [2048, 1024], P('tp', 'shard'), may hold values from -0.1875 to 0.1875
- hidden_gain: float32 [1024], replicated, may hold values from 0.5 to 1.5
- hidden_gate: bfloat16 [1024, 2816], P('shard', 'tp'), may hold values from -0.1875 to 0.1875
- hidden_up: bfloat16 [1024, 2816], P('shard', 'tp'), may hold values from -0.1875 to 0.1875
- hidden_down: bfloat16 [2816, 1024], P('tp', 'shard'), may hold values from -0.15625 to 0.15625
Outputs:
- block_out: bfloat16 [8192, 1024], P(('shard', 'ctx'))
- input_grad: float32 [8192, 1024], P(('shard', 'ctx'))
- mixer_gain_grad: float32 [1024], replicated
- query_weight_grad: float32 [1024, 1024], P('shard', 'tp')
- key_weight_grad: float32 [1024, 1024], P('shard', 'tp')
- value_weight_grad: float32 [1024, 2048], P('shard', 'tp')
- gate_weight_grad: float32 [1024, 2048], P('shard', 'tp')
- decay_weight_grad: float32 [1024, 8], P('shard', 'tp')
- beta_weight_grad: float32 [1024, 8], P('shard', 'tp')
- query_conv_grad: float32 [4, 1024], P(None, 'tp')
- key_conv_grad: float32 [4, 1024], P(None, 'tp')
- value_conv_grad: float32 [4, 2048], P(None, 'tp')
- decay_log_grad: float32 [8], P('tp')
- decay_bias_grad: float32 [8], P('tp')
- out_gain_grad: float32 [256], replicated
- output_weight_grad: float32 [2048, 1024], P('tp', 'shard')
- hidden_gain_grad: float32 [1024], replicated
- hidden_gate_grad: float32 [1024, 2816], P('shard', 'tp')
- hidden_up_grad: float32 [1024, 2816], P('shard', 'tp')
- hidden_down_grad: float32 [2816, 1024], P('tp', 'shard')
Inputs may be any that keep to these rules, and one draw needn't show every extreme that they name: `segment_ids`: within each packed row the document numbers never fall; each document has 1 to 1024 tokens and one has exactly 1024.
All inputs are finite; a program needn't handle non-finite values.
Results may differ from a plain program's by a relative error of at most 0.015.
The roundings to bfloat16 on the way count: a program that leaves them out, or rounds other values in their place, can miss the bound.
Values may be sent and summed in bfloat16 or wider, within the bound.
A program may use at most 256 MiB of HBM per device.

v0:
```python
import jax
import jax.numpy as jnp
from jax import lax
from jax.sharding import PartitionSpec as P

GROUP = 128
HIGH = lax.Precision.HIGHEST
PRECISE = lax.Precision.HIGH


def from_behind(block, axis, distance):
    devices = range(lax.axis_size(axis))
    route = [(i - distance, i) for i in devices if i - distance in devices]
    return lax.ppermute(block, axis, route)


def dot_plain(left, right):
    return jnp.dot(left, right, preferred_element_type=jnp.float32)


def dot_first(left, right):
    return lax.dot_general(
        left, right, (((0,), (0,)), ((), ())), preferred_element_type=jnp.float32
    )


def dot_second(left, right):
    return lax.dot_general(
        left, right, (((1,), (1,)), ((), ())), preferred_element_type=jnp.float32
    )


def rms_norm(values, gain):
    return values * lax.rsqrt(jnp.mean(values * values, axis=-1, keepdims=True) + 1e-06) * gain


def unit_rows(values):
    return values * lax.rsqrt(jnp.sum(values * values, axis=-1, keepdims=True) + 1e-06)


def convolve(projected, rim_rows, weights, seg_ext):
    tok_rows = projected.shape[0]
    taps = weights.shape[0]
    extended = jnp.concatenate([rim_rows, projected], axis=0)
    seg_now = seg_ext[taps - 1 :]
    summed = jnp.zeros_like(projected)
    for offset in range(taps):
        begin = taps - 1 - offset
        linked = (seg_ext[begin : begin + tok_rows] == seg_now).astype(jnp.float32)
        summed = summed + weights[offset] * extended[begin : begin + tok_rows] * linked[:, None]
    return jax.nn.silu(summed)


def dot_high(equation, left, right):
    return jnp.einsum(equation, left, right, precision=PRECISE)


@jax.custom_vjp
def unit_lower_inverse(strict_part):
    size = strict_part.shape[-1]
    order = jnp.arange(size)
    above, across = (order[:, None], order[None, :])
    inverse = jnp.broadcast_to(jnp.eye(size, dtype=jnp.float32), strict_part.shape)
    width = 1
    while width < size:
        paired = (above // (2 * width) == across // (2 * width)) & (
            above // width != across // width
        )
        coupling = jnp.where(paired, strict_part, 0.0)
        if width > 1:
            coupling = dot_high("...ij,...jk->...ik", coupling, inverse)
            coupling = dot_high("...ij,...jk->...ik", inverse, coupling)
        inverse = inverse - coupling
        width *= 2
    return inverse


def inverse_keep(strict_part):
    inverse = unit_lower_inverse(strict_part)
    return (inverse, inverse)


def inverse_pull(inverse, grad):
    inner = dot_high("...ij,...kj->...ik", grad, inverse)
    return (-dot_high("...ji,...jk->...ik", inverse, inner),)


unit_lower_inverse.defvjp(inverse_keep, inverse_pull)


def prepare(floats, seg_ext, key_dim, block_len):
    (
        q_proj,
        k_proj,
        v_proj,
        q_rim,
        k_rim,
        v_rim,
        a_proj,
        b_proj,
        q_conv,
        k_conv,
        v_conv,
        decay_log,
        decay_bias,
    ) = floats
    tok_rows = q_proj.shape[0]
    num_heads = a_proj.shape[1]
    taps = q_conv.shape[0]
    blocks = tok_rows // block_len

    def split(array):
        shaped = array.reshape(blocks, block_len, num_heads, -1)
        return jnp.transpose(shaped, (2, 0, 1, 3))

    query = unit_rows(split(convolve(q_proj, q_rim, q_conv, seg_ext))) * key_dim ** (-0.5)
    keys = unit_rows(split(convolve(k_proj, k_rim, k_conv, seg_ext)))
    values = split(convolve(v_proj, v_rim, v_conv, seg_ext))
    val_dim = values.shape[3]
    beta = jax.nn.sigmoid(b_proj).T.reshape(num_heads, blocks, block_len)
    log_gate = (-jnp.exp(decay_log) * jax.nn.softplus(a_proj + decay_bias)).T
    log_gate = log_gate.reshape(num_heads, blocks, block_len)
    seg_now = seg_ext[taps - 1 :].reshape(blocks, block_len)
    seg_before = seg_ext[taps - 2 : taps - 2 + tok_rows : block_len]
    order = jnp.arange(block_len)
    until = (order[:, None] <= order[None, :]).astype(jnp.float32)
    cumul = jnp.einsum("hcs,st->hct", log_gate, until, precision=HIGH)
    causal = (order[:, None] >= order[None, :]) & (seg_now[:, :, None] == seg_now[:, None, :])
    strict = causal & (order[:, None] > order[None, :])
    spacing = cumul[..., :, None] - cumul[..., None, :]
    within = jnp.where(causal, jnp.exp(jnp.where(causal, spacing, 0.0)), 0.0)
    from_start = jnp.where(seg_now == seg_before[:, None], jnp.exp(cumul), 0.0)
    to_end = within[..., -1, :]
    key_dots = dot_high("hctd,hcsd->hcts", keys, keys)
    inverse = unit_lower_inverse(jnp.where(strict, beta[..., None] * within * key_dots, 0.0))
    scores = dot_high("hctd,hcsd->hcts", query, keys) * within
    sources = jnp.concatenate(
        [(beta * from_start)[..., None] * keys, beta[..., None] * values], axis=-1
    )
    solved = dot_high("hcts,hcsx->hctx", inverse, sources)
    reached = dot_high("hcts,hcsx->hctx", scores, solved)
    moved = dot_high("hctx,hctd->hcxd", solved, keys * to_end[..., None])
    eye = jnp.eye(key_dim, dtype=jnp.float32)
    step_map = from_start[..., -1][..., None, None] * eye - moved[:, :, :key_dim]
    step_base = jnp.concatenate(
        [jnp.zeros((num_heads, blocks, key_dim, key_dim), jnp.float32), moved[:, :, key_dim:]],
        axis=2,
    )
    state = jnp.concatenate(
        [
            jnp.broadcast_to(eye, (num_heads, key_dim, key_dim)),
            jnp.zeros((num_heads, val_dim, key_dim), jnp.float32),
        ],
        axis=1,
    )
    states = []
    for block in range(blocks):
        states.append(state)
        state = dot_high("hxd,hde->hxe", state, step_map[:, block]) + step_base[:, block]
    entry = jnp.stack(states, axis=1)
    reading = from_start[..., None] * query - reached[..., :key_dim]
    outputs = dot_high("hctd,hcxd->hctx", reading, entry)
    mapped = outputs[..., :key_dim].reshape(num_heads, tok_rows, key_dim)
    base = (outputs[..., key_dim:] + reached[..., key_dim:]).reshape(num_heads, tok_rows, val_dim)
    return (mapped, base, state[:, :key_dim], state[:, key_dim:])


def gated_out(core, gate_proj, gain):
    num_heads, tok_rows, val_dim = core.shape
    gating = jax.nn.silu(gate_proj.reshape(tok_rows, num_heads, val_dim))
    normed = rms_norm(core, gain)
    return (jnp.transpose(normed, (1, 0, 2)) * gating).reshape(tok_rows, -1)


def swish_product(gate_pre, up_pre):
    return jax.nn.silu(gate_pre) * up_pre


def add_tail(grad_rows, incoming):
    width = incoming.shape[0]
    return jnp.concatenate([grad_rows[:-width], grad_rows[-width:] + incoming], axis=0)


def body(
    tokens,
    segment_ids,
    cotangent,
    mixer_gain,
    query_weight,
    key_weight,
    value_weight,
    gate_weight,
    decay_weight,
    beta_weight,
    query_conv,
    key_conv,
    value_conv,
    decay_log,
    decay_bias,
    out_gain,
    output_weight,
    hidden_gain,
    hidden_gate,
    hidden_up,
    hidden_down,
):
    tok_rows = tokens.shape[0]
    num_heads = decay_log.shape[0]
    key_dim = query_weight.shape[1] // num_heads
    taps = query_conv.shape[0]
    range_count = lax.axis_size("ctx")
    begin_row = lax.axis_index("ctx") * tok_rows
    seg_pad = jnp.concatenate([jnp.full((taps - 1,), -1, jnp.int32), segment_ids[0]])
    seg_ext = lax.dynamic_slice_in_dim(seg_pad, begin_row, tok_rows + taps - 1)
    low = jnp.bfloat16
    heads_wide = num_heads * key_dim
    values_wide = value_weight.shape[1]
    mixer_wide = 2 * heads_wide + 2 * values_wide
    narrow_pad = jnp.zeros((query_weight.shape[0], -2 * num_heads % 128), low)
    mixer_full = lax.all_gather(
        jnp.concatenate(
            [
                query_weight,
                key_weight,
                value_weight,
                gate_weight,
                decay_weight,
                beta_weight,
                narrow_pad,
            ],
            axis=1,
        ),
        "shard",
        axis=0,
        tiled=True,
    )
    units = hidden_gate.shape[1]
    output_full = lax.all_gather(output_weight.T, "shard", axis=0, tiled=True)
    inner_full = lax.all_gather(
        jnp.concatenate([hidden_gate, hidden_up], axis=1), "shard", axis=0, tiled=True
    )
    down_full = lax.all_gather(hidden_down.T, "shard", axis=0, tiled=True)
    part_rows = tok_rows // lax.axis_size("tp")
    part_at = lax.axis_index("tp") * part_rows

    def own_rows(array):
        return lax.dynamic_slice_in_dim(array, part_at, part_rows)

    def sum_rows(array):
        summed = lax.psum_scatter(array.astype(low), "tp", scatter_dimension=0, tiled=True)
        return summed.astype(jnp.float32)

    def all_rows(array):
        return lax.all_gather(array, "tp", axis=0, tiled=True)

    normed_low = rms_norm(tokens.astype(jnp.float32), mixer_gain).astype(low)
    x_own = own_rows(tokens).astype(jnp.float32)
    _, norm_pull = jax.vjp(rms_norm, x_own, mixer_gain)
    projected = dot_plain(normed_low, mixer_full)
    q_proj = projected[:, :heads_wide]
    k_proj = projected[:, heads_wide : 2 * heads_wide]
    v_proj = projected[:, 2 * heads_wide : 2 * heads_wide + values_wide]
    z_proj = projected[:, 2 * heads_wide + values_wide : mixer_wide]
    a_proj = projected[:, mixer_wide : mixer_wide + num_heads]
    b_proj = projected[:, mixer_wide + num_heads : mixer_wide + 2 * num_heads]
    rim = from_behind(projected[tok_rows - taps + 1 :, : 2 * heads_wide + values_wide], "ctx", 1)
    q_rim = rim[:, :heads_wide]
    k_rim = rim[:, heads_wide : 2 * heads_wide]
    v_rim = rim[:, 2 * heads_wide :]

    def local_mixer(floats):
        return prepare(floats, seg_ext, key_dim, GROUP)

    (mapped_query, base_query, state_map, state_base), prep_pull = jax.vjp(
        local_mixer,
        (
            q_proj,
            k_proj,
            v_proj,
            q_rim,
            k_rim,
            v_rim,
            a_proj,
            b_proj,
            query_conv,
            key_conv,
            value_conv,
            decay_log,
            decay_bias,
        ),
    )
    state_in = jnp.zeros_like(state_base)
    for _ in range(range_count - 1):
        ends = dot_high("hvd,hde->hve", state_in, state_map) + state_base
        state_in = from_behind(ends, "ctx", 1)
    core = base_query + dot_high("hrd,hvd->hrv", mapped_query, state_in)
    mixed, post_pull = jax.vjp(gated_out, core, z_proj, out_gain)
    mixed_low = mixed.astype(low)
    middle = x_own + sum_rows(dot_second(mixed_low, output_full))
    normed2, norm2_pull = jax.vjp(rms_norm, middle, hidden_gain)
    normed2_low = all_rows(normed2.astype(low))
    inner = dot_plain(normed2_low, inner_full)
    act, act_pull = jax.vjp(swish_product, inner[:, :units], inner[:, units:])
    act_low = act.astype(low)
    grad_act = dot_plain(cotangent, down_full)
    grad_gate, grad_up = act_pull(grad_act)
    inner_low = jnp.concatenate([grad_gate.astype(low), grad_up.astype(low)], axis=1)
    grad_normed2 = sum_rows(dot_second(inner_low, inner_full))
    ffn = sum_rows(dot_second(act_low, down_full))
    block_out = all_rows((middle + ffn).astype(low))
    grad_down = dot_first(cotangent, act_low)
    grad_inner = dot_first(normed2_low, inner_low)
    grad_mid_norm, grad_hidden_gain = norm2_pull(grad_normed2)
    grad_middle = own_rows(cotangent).astype(jnp.float32) + grad_mid_norm
    attn_low = all_rows(grad_middle.astype(low))
    grad_output = dot_first(attn_low, mixed_low)
    grad_mixed = dot_plain(attn_low, output_full)
    grad_core, grad_z, grad_out_gain = post_pull(grad_mixed)
    direct = dot_high("hrv,hrd->hvd", grad_core, mapped_query)
    grad_end = jnp.zeros_like(direct)
    for _ in range(range_count - 1):
        totals = dot_high("hve,hde->hvd", grad_end, state_map) + direct
        grad_end = from_behind(totals.astype(low), "ctx", -1).astype(totals.dtype)
    grad_mapped = dot_high("hrv,hvd->hrd", grad_core, state_in)
    grad_map = dot_high("hvd,hve->hde", state_in, grad_end)
    (float_grads,) = prep_pull((grad_mapped, grad_core, grad_map, grad_end))
    (
        grad_q,
        grad_k,
        grad_v,
        grad_q_rim,
        grad_k_rim,
        grad_v_rim,
        grad_a,
        grad_b,
        grad_q_conv,
        grad_k_conv,
        grad_v_conv,
        grad_decay_log,
        grad_decay_bias,
    ) = float_grads
    back_rim = from_behind(jnp.concatenate([grad_q_rim, grad_k_rim, grad_v_rim], axis=1), "ctx", -1)
    conv_grad = add_tail(jnp.concatenate([grad_q, grad_k, grad_v], axis=1), back_rim)
    mixer_low = jnp.concatenate(
        [
            conv_grad.astype(low),
            grad_z.astype(low),
            grad_a.astype(low),
            grad_b.astype(low),
            jnp.zeros((tok_rows, narrow_pad.shape[1]), low),
        ],
        axis=1,
    )
    grad_normed = sum_rows(dot_second(mixer_low, mixer_full))
    grad_mixer = dot_first(normed_low, mixer_low)
    grad_x_norm, grad_mixer_gain = norm_pull(grad_normed)
    input_grad = all_rows((grad_middle + grad_x_norm).astype(low)).astype(jnp.float32)

    def sum_weight(array):
        part = lax.psum_scatter(array.astype(low), "shard", scatter_dimension=0, tiled=True)
        return lax.psum(part, "ctx").astype(jnp.float32)

    sum_inner = sum_weight(jnp.concatenate([grad_inner, grad_down, grad_output], axis=1))
    sum_mixer = sum_weight(grad_mixer)
    sum_mixer_gain, sum_hidden_gain, sum_out_gain = lax.psum(
        (grad_mixer_gain, grad_hidden_gain, grad_out_gain), ("shard", "ctx", "tp")
    )
    sum_q_conv, sum_k_conv, sum_v_conv, sum_decay_log, sum_decay_bias = lax.psum(
        (grad_q_conv, grad_k_conv, grad_v_conv, grad_decay_log, grad_decay_bias), ("shard", "ctx")
    )
    return (
        block_out,
        input_grad,
        sum_mixer_gain,
        sum_mixer[:, :heads_wide],
        sum_mixer[:, heads_wide : 2 * heads_wide],
        sum_mixer[:, 2 * heads_wide : 2 * heads_wide + values_wide],
        sum_mixer[:, 2 * heads_wide + values_wide : mixer_wide],
        sum_mixer[:, mixer_wide : mixer_wide + num_heads],
        sum_mixer[:, mixer_wide + num_heads : mixer_wide + 2 * num_heads],
        sum_q_conv,
        sum_k_conv,
        sum_v_conv,
        sum_decay_log,
        sum_decay_bias,
        sum_out_gain,
        sum_inner[:, 3 * units :].T,
        sum_hidden_gain,
        sum_inner[:, :units],
        sum_inner[:, units : 2 * units],
        sum_inner[:, 2 * units : 3 * units].T,
    )


def solution(mesh):
    in_specs = (
        P(("shard", "ctx"), None),
        P("shard", None),
        P(("shard", "ctx"), None),
        P(),
        P("shard", "tp"),
        P("shard", "tp"),
        P("shard", "tp"),
        P("shard", "tp"),
        P("shard", "tp"),
        P("shard", "tp"),
        P(None, "tp"),
        P(None, "tp"),
        P(None, "tp"),
        P("tp"),
        P("tp"),
        P(),
        P("tp", "shard"),
        P(),
        P("shard", "tp"),
        P("shard", "tp"),
        P("tp", "shard"),
    )
    out_specs = (
        P(("shard", "ctx"), None),
        P(("shard", "ctx"), None),
        P(),
        P("shard", "tp"),
        P("shard", "tp"),
        P("shard", "tp"),
        P("shard", "tp"),
        P("shard", "tp"),
        P("shard", "tp"),
        P(None, "tp"),
        P(None, "tp"),
        P(None, "tp"),
        P("tp"),
        P("tp"),
        P(),
        P("tp", "shard"),
        P(),
        P("shard", "tp"),
        P("shard", "tp"),
        P("tp", "shard"),
    )
    return jax.shard_map(body, mesh=mesh, in_specs=in_specs, out_specs=out_specs, check_vma=False)
```

profile of v0, /device:TPU:0, one launch (start us, length us, event | category | flops | bytes accessed | tf_op | source)
XLA Modules:
  0.0 910.6 jit_solution(14726343507014059583)
XLA Ops:
  17.4 42.8 %all-gather.9.cloned.1.call-done = bf16[1024,1664]{1,0:T(8,128)(2,1)} async-done(((bf16[256,1664]{1,0:T(8,128)(2,1)}), bf16[1024,1664]{1,0:T(8,128)(2,1)}) %all-gather.9.cloned.1.call-update) | async-done | bytes 3407888 | tf_op jit(solution)/shard_map/all_gather | solution.py:220
  60.2 6.0 fusion.105
  101.2 3.1 fusion.37
  104.3 3.6 reshape.824
  111.7 3.2 fusion.89
  124.6 2.7 reshape.820
  141.2 3.0 copy.219
  144.2 3.1 multiply_reduce_fusion.5
  150.3 4.3 convolution_convert_fusion.4
  156.7 41.9 %reduce-scatter.7.cloned.1.call-done = bf16[256,1024]{1,0:T(8,128)(2,1)} async-done(((bf16[1024,1024]{1,0:T(8,128)(2,1)}), bf16[256,1024]{1,0:T(8,128)(2,1)}) %reduce-scatter.7.cloned.1.call-update) | async-done | bytes 524304 | tf_op jit(solution)/shard_map/reduce_scatter | solution.py:250
  204.1 37.8 %all-gather.15.cloned.1.call-done = bf16[1024,1408]{0,1:T(8,128)(2,1)} async-done(((bf16[256,1408]{0,1:T(8,128)(2,1)}), bf16[1024,1408]{0,1:T(8,128)(2,1)}) %all-gather.15.cloned.1.call-update) | async-done | bytes 2883600 | tf_op jit(solution)/shard_map/all_gather | solution.py:239
  242.0 48.0 %all-gather.13.cloned.1.call-done = bf16[1024,1024]{1,0:T(8,128)(2,1)} async-done(((bf16[256,1024]{1,0:T(8,128)(2,1)}), bf16[1024,1024]{1,0:T(8,128)(2,1)}) %all-gather.13.cloned.1.call-update) | async-done | bytes 2097168 | tf_op jit(solution)/shard_map/all_gather | solution.py:254
  290.0 8.4 fusion.265
  298.5 21.9 %all-gather.17.cloned.1.call-done = bf16[1024,704]{0,1:T(8,128)(2,1)} async-done(((bf16[256,704]{0,1:T(8,128)(2,1)}), bf16[1024,704]{0,1:T(8,128)(2,1)}) %all-gather.17.cloned.1.call-update) | async-done | bytes 1441808 | tf_op jit(solution)/shard_map/all_gather | solution.py:242
  320.3 7.7 fusion.5
  329.8 4.7 convolution_convert_fusion.3
  334.6 44.0 %reduce-scatter.11.cloned.1.call-done = bf16[256,1024]{1,0:T(8,128)(2,1)} async-done(((bf16[1024,1024]{1,0:T(8,128)(2,1)}), bf16[256,1024]{1,0:T(8,128)(2,1)}) %reduce-scatter.11.cloned.1.call-update) | async-done | bytes 524304 | tf_op jit(solution)/shard_map/reduce_scatter | solution.py:250
  382.4 2.7 fusion.246
  387.7 42.9 %all-gather.21.cloned.1.call-done = bf16[1024,1024]{1,0:T(8,128)(2,1)} async-done(((bf16[256,1024]{1,0:T(8,128)(2,1)}), bf16[1024,1024]{1,0:T(8,128)(2,1)}) %all-gather.21.cloned.1.call-update) | async-done | bytes 2097168 | tf_op jit(solution)/shard_map/all_gather | solution.py:254
  430.6 5.6 fusion.32
  442.7 2.8 fusion.266
  445.5 2.7 copy.226
  451.4 6.0 fusion.264
  457.5 2.8 fusion.18
  461.3 3.2 fusion.97
  469.5 3.5 multiply_reduce_fusion.18
  475.0 3.0 fusion.6
  512.6 3.2 convolution_add_fusion.3
  518.6 3.4 multiply_reduce_fusion.16
  553.4 5.8 concatenate.60
  559.1 8.4 convolution_convert_fusion.2
  568.9 3.1 convolution_convert_fusion.5
  573.6 7.7 convolution_convert_fusion
  581.4 4.9 fusion.39
  586.2 2.7 copy.275
  588.9 7.7 convolution_convert_fusion.1
  598.9 9.0 concatenate.61
  608.6 3.1 reduce-scatter.13.cloned.1.call-done
  613.2 43.9 %reduce-scatter.9.cloned.1.call-done = bf16[256,1024]{1,0:T(8,128)(2,1)} async-done(((bf16[1024,1024]{1,0:T(8,128)(2,1)}), bf16[256,1024]{1,0:T(8,128)(2,1)}) %reduce-scatter.9.cloned.1.call-update) | async-done | bytes 524304 | tf_op jit(solution)/shard_map/reduce_scatter | solution.py:250
  657.2 3.1 fusion.59
  660.9 44.8 %reduce-scatter.15.cloned.1.call-done = bf16[256,1664]{1,0:T(8,128)(2,1)} async-done(((bf16[1024,1664]{1,0:T(8,128)(2,1)}), bf16[256,1664]{1,0:T(8,128)(2,1)}) %reduce-scatter.15.cloned.1.call-update) | async-done | bytes 851984 | tf_op jit(solution)/shard_map/reduce_scatter | solution.py:360
  705.7 66.6 %reduce-scatter.17.cloned.1.call-done = bf16[256,2624]{1,0:T(8,128)(2,1)} async-done(((bf16[1024,2624]{1,0:T(8,128)(2,1)}), bf16[256,2624]{1,0:T(8,128)(2,1)}) %reduce-scatter.17.cloned.1.call-update) | async-done | bytes 1343504 | tf_op jit(solution)/shard_map/reduce_scatter | solution.py:360
  772.4 24.5 %all-reduce.53 = (f32[4,256]{1,0:T(4,128)}, f32[4,256]{1,0:T(4,128)}, f32[4,512]{1,0:T(4,128)}, f32[2]{0:T(128)}, f32[2]{0:T(128)}) all-reduce(f32[4,256]{1,0:T(4,128)S(1)} %pad_add_fusion.21, f32[4,256]{1,0:T(4,128)S(1)} %pad_add_fusion.20, ...), channel_id=1, replica_groups=mesh['shard'=4,'ctx'=2,'tp'=4] {'shard','ctx'}, use_global_device_ids=true, to_apply=%region_31.32 | all-reduce | flops 4100 | bytes 32800 | tf_op jit(solution)/shard_map/psum | solution.py:368
  796.9 41.0 %all-reduce.52 = (f32[1024]{0:T(1024)}, f32[256]{0:T(256)}, f32[1024]{0:T(1024)}) all-reduce(f32[1024]{0:T(1024)S(1)} %get-tuple-element.89, f32[256]{0:T(256)S(1)} %copy-done.167, f32[1024]{0:T(1024)S(1)} %copy-done.136), channel_id=1, replica_groups=mesh['shard'=4,'ctx'=2,'tp'=4] {'shard','ctx','tp'}, use_global_device_ids=true, to_apply=%region_24.25 | all-reduce | flops 2304 | bytes 18432 | tf_op jit(solution)/shard_map/psum | solution.py:365
  837.8 4.1 convert_element_type.158
  841.9 25.7 %all-gather.19.cloned.1.call-done = bf16[1024,1024]{1,0:T(8,128)(2,1)} async-done(((bf16[256,1024]{1,0:T(8,128)(2,1)}), bf16[1024,1024]{1,0:T(8,128)(2,1)}) %all-gather.19.cloned.1.call-update) | async-done | bytes 2097168 | tf_op jit(solution)/shard_map/all_gather | solution.py:254
  867.6 22.5 %all-reduce.57.cloned.1.call-done = (bf16[256,1664]{1,0:T(8,128)(2,1)}, bf16[256,2624]{1,0:T(8,128)(2,1)}) async-done(((bf16[256,1664]{1,0:T(8,128)(2,1)}, bf16[256,2624]{1,0:T(8,128)(2,1)}), (bf16[256,1664]{1,0:T(8,128)(2,1)}, bf16[256,2624]{1,0:T(8,128)(2,1)})) %all-reduce.57.cloned.1.call-update) | async-done | bytes 2195472 | tf_op jit(solution)/shard_map/psum | solution.py:361
  900.8 3.1 copy.398
  (596 shorter events, 194.2 us)
Async XLA Ops:
  7.2 53.0 %all-gather.9.cloned.1.call-start = ((), (), s32[]{:S(2)}) async-start(), calls=%async_computation.6 | async-start | bytes 4259840 | tf_op jit(solution)/shard_map/all_gather | solution.py:220
  11.2 49.0 %copy-start.134 = (f32[1024]{0:T(1024)S(1)}, f32[1024]{0:T(1024)}, u32[]{:S(2)}) copy-start(f32[1024]{0:T(1024)} %param.24) | copy-start | bytes 12292
  11.2 139.1 %all-gather.11.cloned.1.call-start = ((), (), s32[]{:S(2)}) async-start(), calls=%async_computation.7 | async-start | bytes 1310720 | tf_op jit(solution)/shard_map/all_gather | solution.py:238
  11.9 186.6 %reduce-scatter.7.cloned.1.call-start = ((), (), s32[]{:S(2)}) async-start(), calls=%async_computation.8 | async-start | bytes 2621440 | tf_op jit(solution)/shard_map/reduce_scatter | solution.py:250
  12.1 103.0 %copy-start.75 = (f32[128,128]{1,0:T(8,128)}, f32[128,128]{1,0:T(8,128)S(1)}, u32[]{:S(2)}) copy-start(f32[128,128]{1,0:T(8,128)S(1)} %fusion.183) | copy-start | bytes 196612
  12.6 53.6 %copy-start.172 = (f32[1024]{0:T(1024)}, f32[1024]{0:T(1024)S(1)}, u32[]{:S(2)}) copy-start(f32[1024]{0:T(1024)S(1)} %add_rsqrt_fusion.2) | copy-start | bytes 12292
  13.2 65.6 %copy-start.148 = (f32[1,256]{1,0:T(1,128)}, f32[1,256]{1,0:T(1,128)S(1)}, u32[]{:S(2)}) copy-start(f32[1,256]{1,0:T(1,128)S(1)} %get-tuple-element.196) | copy-start | bytes 3076
  13.2 65.6 %copy-start.150 = (f32[1,256]{1,0:T(1,128)}, f32[1,256]{1,0:T(1,128)S(1)}, u32[]{:S(2)}) copy-start(f32[1,256]{1,0:T(1,128)S(1)} %get-tuple-element.197) | copy-start | bytes 3076
  13.4 59.5 %copy-start.176 = (f32[2]{0:T(128)}, f32[2]{0:T(128)S(1)}, u32[]{:S(2)}) copy-start(f32[2]{0:T(128)S(1)} %exponential_negate_fusion) | copy-start | bytes 28
  14.0 87.1 %copy-start.126 = (f32[1,512]{1,0:T(1,128)}, f32[1,512]{1,0:T(1,128)S(1)}, u32[]{:S(2)}) copy-start(f32[1,512]{1,0:T(1,128)S(1)} %get-tuple-element.185) | copy-start | bytes 6148
  14.1 101.7 %copy-start.71 = (f32[2,128,128]{2,1,0:T(8,128)}, f32[2,128,128]{2,1,0:T(8,128)S(1)}, u32[]{:S(2)}) copy-start(f32[2,128,128]{2,1,0:T(8,128)S(1)} %broadcast_in_dim.210) | copy-start | bytes 393220
  15.6 58.8 %copy-start.162 = (pred[8,128]{1,0:T(8,128)(4,1)}, pred[8,128]{1,0:T(8,128)(4,1)S(1)}, u32[]{:S(2)}) copy-start(pred[8,128]{1,0:T(8,128)(4,1)S(1)} %get-tuple-element.131) | copy-start | bytes 3076
  15.7 85.5 %copy-start.87 = (f32[1024]{0:T(1024)}, f32[1024]{0:T(1024)S(1)}, u32[]{:S(2)}) copy-start(f32[1024]{0:T(1024)S(1)} %get-tuple-element.189) | copy-start | bytes 12292
  15.7 85.5 %copy-start.90 = (f32[1024]{0:T(1024)}, f32[1024]{0:T(1024)S(1)}, u32[]{:S(2)}) copy-start(f32[1024]{0:T(1024)S(1)} %get-tuple-element.190) | copy-start | bytes 12292
  15.7 85.5 %copy-start.93 = (f32[1024]{0:T(1024)}, f32[1024]{0:T(1024)S(1)}, u32[]{:S(2)}) copy-start(f32[1024]{0:T(1024)S(1)} %get-tuple-element.191) | copy-start | bytes 12292
  68.5 10.3 %copy-start.38 = (f32[1024,256]{1,0:T(8,128)}, f32[1024,256]{1,0:T(8,128)S(1)}, u32[]{:S(2)}) copy-start(f32[1024,256]{1,0:T(8,128)S(1)} %get-tuple-element.143) | copy-start | bytes 3145732
  71.2 7.0 collective-permute-start
  74.4 9.3 %copy-start.100 = (f32[1,2,8,128]{3,1,2,0:T(2,128)}, f32[1,2,8,128]{3,1,2,0:T(2,128)S(1)}, u32[]{:S(2)}) copy-start(f32[1,2,8,128]{3,1,2,0:T(2,128)S(1)} %fusion.357) | copy-start | bytes 24580
  75.1 8.5 copy-start.82
  76.2 31.6 %copy-start.80 = (f32[1,2,8,128]{3,2,1,0:T(8,128)}, f32[1,2,8,128]{3,2,1,0:T(8,128)S(1)}, u32[]{:S(2)}) copy-start(f32[1,2,8,128]{3,2,1,0:T(8,128)S(1)} %copy.387) | copy-start | bytes 24580
  76.2 35.4 %copy-start.98 = (f32[2,8,1,128]{3,2,1,0:T(1,128)}, f32[2,8,1,128]{3,2,1,0:T(1,128)S(1)}, u32[]{:S(2)}) copy-start(f32[2,8,1,128]{3,2,1,0:T(1,128)S(1)} %slice.340) | copy-start | bytes 24580
  85.5 12.5 %copy-start.51 = (f32[2,8,128,128]{3,2,1,0:T(8,128)}, f32[2,8,128,128]{3,2,1,0:T(8,128)S(1)}, u32[]{:S(2)}) copy-start(f32[2,8,128,128]{3,2,1,0:T(8,128)S(1)} %fusion.245) | copy-start | bytes 3145732
  120.8 23.4 %collective-permute-start.1 = (f32[2,256,128]{2,1,0:T(8,128)}, f32[2,256,128]{2,1,0:T(8,128)S(1)}, u32[]{:S(2)}, u32[]{:S(2)}) collective-permute-start(f32[2,256,128]{2,1,0:T(8,128)} %convolution_add_fusion.20), channel_id=1, source_target_pairs={{0,4},{1,5},{2,6},{3,7},{8,12},{9,13},{10,14},{11,15},{16,20},{17,... | collective-permute-start | bytes 786440 | tf_op jit(solution)/shard_map/ppermute | solution.py:14
  154.5 87.4 %all-gather.15.cloned.1.call-start = ((), (), s32[]{:S(2)}) async-start(), calls=%async_computation.10 | async-start | bytes 3604480 | tf_op jit(solution)/shard_map/all_gather | solution.py:239
  156.6 133.4 %all-gather.13.cloned.1.call-start = ((), (), s32[]{:S(2)}) async-start(), calls=%async_computation.9 | async-start | bytes 2621440 | tf_op jit(solution)/shard_map/all_gather | solution.py:254
  203.3 117.0 %all-gather.17.cloned.1.call-start = ((), (), s32[]{:S(2)}) async-start(), calls=%async_computation.11 | async-start | bytes 1802240 | tf_op jit(solution)/shard_map/all_gather | solution.py:242
  203.9 174.7 %reduce-scatter.11.cloned.1.call-start = ((), (), s32[]{:S(2)}) async-start(), calls=%async_computation.14 | async-start | bytes 2621440 | tf_op jit(solution)/shard_map/reduce_scatter | solution.py:250
  320.3 9.5 %copy-start.178 = (bf16[1024,1408]{0,1:T(8,128)(2,1)S(1)}, bf16[1024,1408]{0,1:T(8,128)(2,1)}, u32[]{:S(2)}) copy-start(bf16[1024,1408]{0,1:T(8,128)(2,1)} %all-gather.15.cloned.1.call-done) | copy-start | bytes 8650756
  334.6 96.0 %all-gather.21.cloned.1.call-start = ((), (), s32[]{:S(2)}) async-start(), calls=%async_computation.15 | async-start | bytes 2621440 | tf_op jit(solution)/shard_map/all_gather | solution.py:254
  385.1 226.5 %reduce-scatter.13.cloned.1.call-start = ((), (), s32[]{:S(2)}) async-start(), calls=%async_computation.16 | async-start | bytes 2621440 | tf_op jit(solution)/shard_map/reduce_scatter | solution.py:250
  450.1 32.5 %collective-permute-start.2 = (bf16[2,256,128]{2,1,0:T(8,128)(2,1)}, bf16[2,256,128]{2,1,0:T(8,128)(2,1)}, u32[]{:S(2)}, u32[]{:S(2)}) collective-permute-start(bf16[2,256,128]{2,1,0:T(8,128)(2,1)} %fusion.44), channel_id=1, source_target_pairs={{4,0},{5,1},{6,2},{7,3},{12,8},{13,9},{14,10},{15,11},{20,16},{21,... | collective-permute-start | bytes 393224 | tf_op jit(solution)/shard_map/ppermute | solution.py:14
  512.6 11.2 %slice-start = ((s8[6815744]{0:T(1024)(128)(4,1)}), s8[4194304]{0:T(1024)(128)(4,1)S(1)}, s32[]{:S(2)}) async-start(s8[6815744]{0:T(1024)(128)(4,1)} %bitcast.463), calls=%async_computation.21 | async-start | bytes 8388608
  546.6 3.8 collective-permute-start.3
  559.1 8.5 copy-start.184
  567.6 89.6 %reduce-scatter.9.cloned.1.call-start = ((), (), s32[]{:S(2)}) async-start(), calls=%async_computation.12 | async-start | bytes 2621440 | tf_op jit(solution)/shard_map/reduce_scatter | solution.py:250
  572.1 133.7 %reduce-scatter.15.cloned.1.call-start = ((), (), s32[]{:S(2)}) async-start(), calls=%async_computation.18 | async-start | bytes 4259840 | tf_op jit(solution)/shard_map/reduce_scatter | solution.py:360
  581.3 191.0 %reduce-scatter.17.cloned.1.call-start = ((), (), s32[]{:S(2)}) async-start(), calls=%async_computation.19 | async-start | bytes 6881280 | tf_op jit(solution)/shard_map/reduce_scatter | solution.py:360
  607.9 49.2 %copy-start.24 = (bf16[256,1024]{1,0:T(8,128)(2,1)S(1)}, bf16[256,1024]{1,0:T(8,128)(2,1)}, u32[]{:S(2)}) copy-start(bf16[256,1024]{1,0:T(8,128)(2,1)} %reduce-scatter.7.cloned.1.call-done) | copy-start | bytes 1572868
  607.9 49.2 %copy-start.49 = (bf16[256,1024]{1,0:T(8,128)(2,1)S(1)}, bf16[256,1024]{1,0:T(8,128)(2,1)}, u32[]{:S(2)}) copy-start(bf16[256,1024]{1,0:T(8,128)(2,1)} %reduce-scatter.11.cloned.1.call-done) | copy-start | bytes 1572868
  607.9 49.2 %copy-start.115 = (f32[1024]{0:T(1024)S(1)}, f32[1024]{0:T(1024)}, u32[]{:S(2)}) copy-start(f32[1024]{0:T(1024)} %param.38) | copy-start | bytes 12292
  608.0 49.2 %copy-start.123 = (f32[256]{0:T(256)S(1)}, f32[256]{0:T(256)}, u32[]{:S(2)}) copy-start(f32[256]{0:T(256)} %copy-done.122) | copy-start | bytes 3076
  608.0 49.2 %copy-start.147 = (f32[256]{0:T(256)S(1)}, f32[256]{0:T(256)}, u32[]{:S(2)}) copy-start(f32[256]{0:T(256)} %copy-done.146) | copy-start | bytes 3076
  608.0 229.8 %all-gather.23.cloned.1.call-start = ((), (), s32[]{:S(2)}) async-start(), calls=%async_computation.17 | async-start | bytes 2621440 | tf_op jit(solution)/shard_map/all_gather | solution.py:254
  660.3 112.1 %copy-start.181 = (f32[2]{0:T(128)S(1)}, f32[2]{0:T(128)}, u32[]{:S(2)}) copy-start(f32[2]{0:T(128)} %param.34) | copy-start | bytes 28
  660.3 136.6 %copy-start.136 = (f32[1024]{0:T(1024)S(1)}, f32[1024]{0:T(1024)}, u32[]{:S(2)}) copy-start(f32[1024]{0:T(1024)} %get-tuple-element.87) | copy-start | bytes 12292
  660.3 136.6 %copy-start.167 = (f32[256]{0:T(256)S(1)}, f32[256]{0:T(256)}, u32[]{:S(2)}) copy-start(f32[256]{0:T(256)} %get-tuple-element.82) | copy-start | bytes 3076
  660.3 207.3 %all-gather.19.cloned.1.call-start = ((), (), s32[]{:S(2)}) async-start(), calls=%async_computation.13 | async-start | bytes 2621440 | tf_op jit(solution)/shard_map/all_gather | solution.py:254
  660.9 229.2 %all-reduce.57.cloned.1.call-start = ((), (), s32[]{:S(2)}) async-start(), calls=%async_computation.20 | async-start | bytes 4456448 | tf_op jit(solution)/shard_map/psum | solution.py:361
  (158 other events, 385.1 us)
Sparse Core Ops, SparseCore 0:
  11.3 48.8 all-gather.8
  62.0 26.4 all-gather.10
  154.7 43.8 reduce-scatter.6
  201.0 40.9 all-gather.14
  244.0 45.9 all-gather.12
  291.8 28.4 all-gather.16
  334.7 43.8 reduce-scatter.10
  385.3 45.2 all-gather.20
  567.7 43.9 reduce-scatter.12
  613.9 43.1 reduce-scatter.8
  660.2 45.4 reduce-scatter.14
  708.6 63.6 reduce-scatter.16
  774.4 46.3 all-gather.22
  822.8 44.7 all-gather.18
  869.9 20.1 all-reduce.56
where the time goes:
time: 920 us; the launch traced here: 911 us
  waiting for transfers between devices  488 us (53%)
  matrix products  160 us (17%)
  local copies, waits for them, and re-layouts  101 us (11%)
  other arithmetic  72.8 us (8%)
  blocking collectives  65.5 us (7%)
  between operations  16.8 us (2%)
    reduce_scatter x4, waiting for transfers between devices, sum_rows(): lax.psum_scatter(array.astype(low), 'tp', scatter_dimension=0, tiled=True)  133 us
    all_gather x4, waiting for transfers between devices, all_rows(): return lax.all_gather(array, 'tp', axis=0, tiled=True)  117 us
    reduce_scatter x2, waiting for transfers between devices, sum_weight(): lax.psum_scatter(array.astype(low), 'shard', scatter_dimension=0, tiled=T...  111 us
    dot_general x59, matrix products, dot_high(): return jnp.einsum(equation, left, right, precision=PRECISE)  86.5 us
    all_gather x1, waiting for transfers between devices, body(): lax.all_gather(jnp.concatenate([query_weight, key_weight, value_weight, g...  42.8 us
    psum x1, blocking collectives, body(): lax.psum((grad_mixer_gain, grad_hidden_gain, grad_out_gain), ('shard', 'c...  41 us
    all_gather x1, waiting for transfers between devices, body(): lax.all_gather(jnp.concatenate([hidden_gate, hidden_up], axis=1), 'shard'...  37.8 us
    unnamed x387, local copies, waits for them, and re-layouts  35.2 us
  transfers between devices with their start and end apart: 19, of which 13 were waited for; matrix products, arithmetic and copies ran while one was open for 20% of the time, Pallas kernels for 0%

commit v1 on v0

--- a/solution.py
+++ b/solution.py
@@ -6,6 +6,12 @@
 GROUP = 128
 HIGH = lax.Precision.HIGHEST
 PRECISE = lax.Precision.HIGH
+
+
+def note_widths_by_axis(payload):
+    for s in ("ctx", "shard"):
+        payload = lax.psum(payload, s)
+    return payload
 
 
 def from_behind(block, axis, distance):
@@ -365,8 +371,8 @@
     sum_mixer_gain, sum_hidden_gain, sum_out_gain = lax.psum(
         (grad_mixer_gain, grad_hidden_gain, grad_out_gain), ("shard", "ctx", "tp")
     )
-    sum_q_conv, sum_k_conv, sum_v_conv, sum_decay_log, sum_decay_bias = lax.psum(
-        (grad_q_conv, grad_k_conv, grad_v_conv, grad_decay_log, grad_decay_bias), ("shard", "ctx")
+    sum_q_conv, sum_k_conv, sum_v_conv, sum_decay_log, sum_decay_bias = note_widths_by_axis(
+        (grad_q_conv, grad_k_conv, grad_v_conv, grad_decay_log, grad_decay_bias)
     )
     return (
         block_out,

time: 920 us -> 920 us (level)
    psum x1 -> x2, blocking collectives: 24.5 us -> 19.2 us  [note_widths_by_axis(): payload = lax.psum(payload, s)]
where the time goes in v1:
time: 920 us; the launch traced here: 911 us
  waiting for transfers between devices  494 us (54%)
  matrix products  160 us (17%)
  local copies, waits for them, and re-layouts  101 us (11%)
  other arithmetic  72.8 us (8%)
  blocking collectives  60 us (7%)
  between operations  16.8 us (2%)
    reduce_scatter x4, waiting for transfers between devices, sum_rows(): lax.psum_scatter(array.astype(low), 'tp', scatter_dimension=0, tiled=True)  133 us
    all_gather x4, waiting for transfers between devices, all_rows(): return lax.all_gather(array, 'tp', axis=0, tiled=True)  122 us
    reduce_scatter x2, waiting for transfers between devices, sum_weight(): lax.psum_scatter(array.astype(low), 'shard', scatter_dimension=0, tiled=T...  111 us
    dot_general x59, matrix products, dot_high(): return jnp.einsum(equation, left, right, precision=PRECISE)  86.5 us
    all_gather x1, waiting for transfers between devices, body(): lax.all_gather(jnp.concatenate([query_weight, key_weight, value_weight, g...  42.8 us
    psum x1, blocking collectives, body(): lax.psum((grad_mixer_gain, grad_hidden_gain, grad_out_gain), ('shard', 'c...  40.8 us
    all_gather x1, waiting for transfers between devices, body(): lax.all_gather(jnp.concatenate([hidden_gate, hidden_up], axis=1), 'shard'...  37.8 us
    unnamed x387, local copies, waits for them, and re-layouts  35.3 us
  transfers between devices with their start and end apart: 19, of which 13 were waited for; matrix products, arithmetic and copies ran while one was open for 20% of the time, Pallas kernels for 0%

profile of v1, /device:TPU:0, one launch (start us, length us, event | category | flops | bytes accessed | tf_op | source)
XLA Modules:
  0.0 910.9 jit_solution(17294539100570969836)
XLA Ops:
  17.4 42.8 %all-gather.9.cloned.1.call-done = bf16[1024,1664]{1,0:T(8,128)(2,1)} async-done(((bf16[256,1664]{1,0:T(8,128)(2,1)}), bf16[1024,1664]{1,0:T(8,128)(2,1)}) %all-gather.9.cloned.1.call-update) | async-done | bytes 3407888 | tf_op jit(solution)/shard_map/all_gather | solution.py:226
  60.2 6.0 fusion.105
  101.2 3.1 fusion.37
  104.3 3.5 reshape.824
  111.7 3.2 fusion.89
  124.6 2.7 reshape.820
  141.1 3.0 copy.219
  144.1 3.1 multiply_reduce_fusion.5
  150.2 4.3 convolution_convert_fusion.4
  156.7 41.9 %reduce-scatter.7.cloned.1.call-done = bf16[256,1024]{1,0:T(8,128)(2,1)} async-done(((bf16[1024,1024]{1,0:T(8,128)(2,1)}), bf16[256,1024]{1,0:T(8,128)(2,1)}) %reduce-scatter.7.cloned.1.call-update) | async-done | bytes 524304 | tf_op jit(solution)/shard_map/reduce_scatter | solution.py:256
  204.2 37.8 %all-gather.15.cloned.1.call-done = bf16[1024,1408]{0,1:T(8,128)(2,1)} async-done(((bf16[256,1408]{0,1:T(8,128)(2,1)}), bf16[1024,1408]{0,1:T(8,128)(2,1)}) %all-gather.15.cloned.1.call-update) | async-done | bytes 2883600 | tf_op jit(solution)/shard_map/all_gather | solution.py:245
  242.0 48.0 %all-gather.13.cloned.1.call-done = bf16[1024,1024]{1,0:T(8,128)(2,1)} async-done(((bf16[256,1024]{1,0:T(8,128)(2,1)}), bf16[1024,1024]{1,0:T(8,128)(2,1)}) %all-gather.13.cloned.1.call-update) | async-done | bytes 2097168 | tf_op jit(solution)/shard_map/all_gather | solution.py:260
  290.0 8.4 fusion.265
  298.5 21.9 %all-gather.17.cloned.1.call-done = bf16[1024,704]{0,1:T(8,128)(2,1)} async-done(((bf16[256,704]{0,1:T(8,128)(2,1)}), bf16[1024,704]{0,1:T(8,128)(2,1)}) %all-gather.17.cloned.1.call-update) | async-done | bytes 1441808 | tf_op jit(solution)/shard_map/all_gather | solution.py:248
  320.3 7.7 fusion.5
  329.8 4.7 convolution_convert_fusion.3
  334.7 44.0 %reduce-scatter.11.cloned.1.call-done = bf16[256,1024]{1,0:T(8,128)(2,1)} async-done(((bf16[1024,1024]{1,0:T(8,128)(2,1)}), bf16[256,1024]{1,0:T(8,128)(2,1)}) %reduce-scatter.11.cloned.1.call-update) | async-done | bytes 524304 | tf_op jit(solution)/shard_map/reduce_scatter | solution.py:256
  382.4 2.7 fusion.246
  387.7 42.9 %all-gather.21.cloned.1.call-done = bf16[1024,1024]{1,0:T(8,128)(2,1)} async-done(((bf16[256,1024]{1,0:T(8,128)(2,1)}), bf16[1024,1024]{1,0:T(8,128)(2,1)}) %all-gather.21.cloned.1.call-update) | async-done | bytes 2097168 | tf_op jit(solution)/shard_map/all_gather | solution.py:260
  430.6 5.6 fusion.32
  442.7 2.8 fusion.266
  445.5 2.7 copy.226
  451.5 6.0 fusion.264
  457.5 2.8 fusion.18
  461.3 3.2 fusion.97
  469.5 3.5 multiply_reduce_fusion.18
  475.0 3.0 fusion.6
  512.6 3.2 convolution_add_fusion.3
  518.5 3.4 multiply_reduce_fusion.16
  553.3 5.8 concatenate.60
  559.1 8.4 convolution_convert_fusion.2
  568.9 3.1 convolution_convert_fusion.5
  573.6 7.7 convolution_convert_fusion
  581.3 4.9 fusion.39
  588.9 7.7 convolution_convert_fusion.1
  598.9 9.0 concatenate.61
  608.5 3.1 reduce-scatter.13.cloned.1.call-done
  613.2 43.9 %reduce-scatter.9.cloned.1.call-done = bf16[256,1024]{1,0:T(8,128)(2,1)} async-done(((bf16[1024,1024]{1,0:T(8,128)(2,1)}), bf16[256,1024]{1,0:T(8,128)(2,1)}) %reduce-scatter.9.cloned.1.call-update) | async-done | bytes 524304 | tf_op jit(solution)/shard_map/reduce_scatter | solution.py:256
  657.1 3.1 fusion.59
  660.9 44.8 %reduce-scatter.15.cloned.1.call-done = bf16[256,1664]{1,0:T(8,128)(2,1)} async-done(((bf16[1024,1664]{1,0:T(8,128)(2,1)}), bf16[256,1664]{1,0:T(8,128)(2,1)}) %reduce-scatter.15.cloned.1.call-update) | async-done | bytes 851984 | tf_op jit(solution)/shard_map/reduce_scatter | solution.py:366
  705.7 66.6 %reduce-scatter.17.cloned.1.call-done = bf16[256,2624]{1,0:T(8,128)(2,1)} async-done(((bf16[1024,2624]{1,0:T(8,128)(2,1)}), bf16[256,2624]{1,0:T(8,128)(2,1)}) %reduce-scatter.17.cloned.1.call-update) | async-done | bytes 1343504 | tf_op jit(solution)/shard_map/reduce_scatter | solution.py:366
  772.3 3.4 all-reduce.54
  775.7 15.8 %all-reduce.53 = (f32[4,256]{1,0:T(4,128)}, f32[4,256]{1,0:T(4,128)}, f32[4,512]{1,0:T(4,128)}, f32[2]{0:T(128)}, f32[2]{0:T(128)}) all-reduce(f32[4,256]{1,0:T(4,128)S(1)} %get-tuple-element.120, f32[4,256]{1,0:T(4,128)S(1)} %get-tuple-element.121, ...), channel_id=1, replica_groups=mesh['shard'=4,'ctx'=2,'tp'=4] {'shard'}, use_global_device_ids=true, to_apply=%region_32.33 | all-reduce | flops 4100 | bytes 32800 | tf_op jit(solution)/shard_map/psum | solution.py:13
  791.6 40.8 %all-reduce.52 = (f32[1024]{0:T(1024)}, f32[256]{0:T(256)}, f32[1024]{0:T(1024)}) all-reduce(f32[1024]{0:T(1024)S(1)} %get-tuple-element.89, f32[256]{0:T(256)S(1)} %copy-done.167, f32[1024]{0:T(1024)S(1)} %copy-done.136), channel_id=1, replica_groups=mesh['shard'=4,'ctx'=2,'tp'=4] {'shard','ctx','tp'}, use_global_device_ids=true, to_apply=%region_24.25 | all-reduce | flops 2304 | bytes 18432 | tf_op jit(solution)/shard_map/psum | solution.py:371
  832.4 4.1 convert_element_type.158
  836.4 31.5 %all-gather.19.cloned.1.call-done = bf16[1024,1024]{1,0:T(8,128)(2,1)} async-done(((bf16[256,1024]{1,0:T(8,128)(2,1)}), bf16[1024,1024]{1,0:T(8,128)(2,1)}) %all-gather.19.cloned.1.call-update) | async-done | bytes 2097168 | tf_op jit(solution)/shard_map/all_gather | solution.py:260
  868.0 22.4 %all-reduce.58.cloned.1.call-done = (bf16[256,1664]{1,0:T(8,128)(2,1)}, bf16[256,2624]{1,0:T(8,128)(2,1)}) async-done(((bf16[256,1664]{1,0:T(8,128)(2,1)}, bf16[256,2624]{1,0:T(8,128)(2,1)}), (bf16[256,1664]{1,0:T(8,128)(2,1)}, bf16[256,2624]{1,0:T(8,128)(2,1)})) %all-reduce.58.cloned.1.call-update) | async-done | bytes 2195472 | tf_op jit(solution)/shard_map/psum | solution.py:367
  901.1 3.1 copy.398
  (597 shorter events, 196.9 us)
Async XLA Ops:
  7.2 53.0 %all-gather.9.cloned.1.call-start = ((), (), s32[]{:S(2)}) async-start(), calls=%async_computation.6 | async-start | bytes 4259840 | tf_op jit(solution)/shard_map/all_gather | solution.py:226
  11.2 49.0 %copy-start.134 = (f32[1024]{0:T(1024)S(1)}, f32[1024]{0:T(1024)}, u32[]{:S(2)}) copy-start(f32[1024]{0:T(1024)} %param.24) | copy-start | bytes 12292
  11.2 139.1 %all-gather.11.cloned.1.call-start = ((), (), s32[]{:S(2)}) async-start(), calls=%async_computation.7 | async-start | bytes 1310720 | tf_op jit(solution)/shard_map/all_gather | solution.py:244
  11.9 186.6 %reduce-scatter.7.cloned.1.call-start = ((), (), s32[]{:S(2)}) async-start(), calls=%async_computation.8 | async-start | bytes 2621440 | tf_op jit(solution)/shard_map/reduce_scatter | solution.py:256
  12.1 103.0 %copy-start.75 = (f32[128,128]{1,0:T(8,128)}, f32[128,128]{1,0:T(8,128)S(1)}, u32[]{:S(2)}) copy-start(f32[128,128]{1,0:T(8,128)S(1)} %fusion.183) | copy-start | bytes 196612
  12.6 53.6 %copy-start.172 = (f32[1024]{0:T(1024)}, f32[1024]{0:T(1024)S(1)}, u32[]{:S(2)}) copy-start(f32[1024]{0:T(1024)S(1)} %add_rsqrt_fusion.2) | copy-start | bytes 12292
  13.2 65.6 %copy-start.148 = (f32[1,256]{1,0:T(1,128)}, f32[1,256]{1,0:T(1,128)S(1)}, u32[]{:S(2)}) copy-start(f32[1,256]{1,0:T(1,128)S(1)} %get-tuple-element.201) | copy-start | bytes 3076
  13.2 65.6 %copy-start.150 = (f32[1,256]{1,0:T(1,128)}, f32[1,256]{1,0:T(1,128)S(1)}, u32[]{:S(2)}) copy-start(f32[1,256]{1,0:T(1,128)S(1)} %get-tuple-element.202) | copy-start | bytes 3076
  13.4 59.5 %copy-start.176 = (f32[2]{0:T(128)}, f32[2]{0:T(128)S(1)}, u32[]{:S(2)}) copy-start(f32[2]{0:T(128)S(1)} %exponential_negate_fusion) | copy-start | bytes 28
  14.0 87.1 %copy-start.126 = (f32[1,512]{1,0:T(1,128)}, f32[1,512]{1,0:T(1,128)S(1)}, u32[]{:S(2)}) copy-start(f32[1,512]{1,0:T(1,128)S(1)} %get-tuple-element.190) | copy-start | bytes 6148
  14.0 101.7 %copy-start.71 = (f32[2,128,128]{2,1,0:T(8,128)}, f32[2,128,128]{2,1,0:T(8,128)S(1)}, u32[]{:S(2)}) copy-start(f32[2,128,128]{2,1,0:T(8,128)S(1)} %broadcast_in_dim.210) | copy-start | bytes 393220
  15.5 58.9 %copy-start.162 = (pred[8,128]{1,0:T(8,128)(4,1)}, pred[8,128]{1,0:T(8,128)(4,1)S(1)}, u32[]{:S(2)}) copy-start(pred[8,128]{1,0:T(8,128)(4,1)S(1)} %get-tuple-element.136) | copy-start | bytes 3076
  15.6 85.5 %copy-start.87 = (f32[1024]{0:T(1024)}, f32[1024]{0:T(1024)S(1)}, u32[]{:S(2)}) copy-start(f32[1024]{0:T(1024)S(1)} %get-tuple-element.194) | copy-start | bytes 12292
  15.6 85.5 %copy-start.90 = (f32[1024]{0:T(1024)}, f32[1024]{0:T(1024)S(1)}, u32[]{:S(2)}) copy-start(f32[1024]{0:T(1024)S(1)} %get-tuple-element.195) | copy-start | bytes 12292
  15.6 85.5 %copy-start.93 = (f32[1024]{0:T(1024)}, f32[1024]{0:T(1024)S(1)}, u32[]{:S(2)}) copy-start(f32[1024]{0:T(1024)S(1)} %get-tuple-element.196) | copy-start | bytes 12292
  68.5 10.3 %copy-start.38 = (f32[1024,256]{1,0:T(8,128)}, f32[1024,256]{1,0:T(8,128)S(1)}, u32[]{:S(2)}) copy-start(f32[1024,256]{1,0:T(8,128)S(1)} %get-tuple-element.148) | copy-start | bytes 3145732
  71.2 7.0 collective-permute-start
  74.4 9.2 %copy-start.100 = (f32[1,2,8,128]{3,1,2,0:T(2,128)}, f32[1,2,8,128]{3,1,2,0:T(2,128)S(1)}, u32[]{:S(2)}) copy-start(f32[1,2,8,128]{3,1,2,0:T(2,128)S(1)} %fusion.357) | copy-start | bytes 24580
  75.2 8.5 copy-start.82
  76.2 31.6 %copy-start.80 = (f32[1,2,8,128]{3,2,1,0:T(8,128)}, f32[1,2,8,128]{3,2,1,0:T(8,128)S(1)}, u32[]{:S(2)}) copy-start(f32[1,2,8,128]{3,2,1,0:T(8,128)S(1)} %copy.387) | copy-start | bytes 24580
  76.3 35.4 %copy-start.98 = (f32[2,8,1,128]{3,2,1,0:T(1,128)}, f32[2,8,1,128]{3,2,1,0:T(1,128)S(1)}, u32[]{:S(2)}) copy-start(f32[2,8,1,128]{3,2,1,0:T(1,128)S(1)} %slice.340) | copy-start | bytes 24580
  85.5 12.5 %copy-start.51 = (f32[2,8,128,128]{3,2,1,0:T(8,128)}, f32[2,8,128,128]{3,2,1,0:T(8,128)S(1)}, u32[]{:S(2)}) copy-start(f32[2,8,128,128]{3,2,1,0:T(8,128)S(1)} %fusion.245) | copy-start | bytes 3145732
  120.8 23.4 %collective-permute-start.1 = (f32[2,256,128]{2,1,0:T(8,128)}, f32[2,256,128]{2,1,0:T(8,128)S(1)}, u32[]{:S(2)}, u32[]{:S(2)}) collective-permute-start(f32[2,256,128]{2,1,0:T(8,128)} %convolution_add_fusion.20), channel_id=1, source_target_pairs={{0,4},{1,5},{2,6},{3,7},{8,12},{9,13},{10,14},{11,15},{16,20},{17,... | collective-permute-start | bytes 786440 | tf_op jit(solution)/shard_map/ppermute | solution.py:20
  154.5 87.4 %all-gather.15.cloned.1.call-start = ((), (), s32[]{:S(2)}) async-start(), calls=%async_computation.10 | async-start | bytes 3604480 | tf_op jit(solution)/shard_map/all_gather | solution.py:245
  156.6 133.4 %all-gather.13.cloned.1.call-start = ((), (), s32[]{:S(2)}) async-start(), calls=%async_computation.9 | async-start | bytes 2621440 | tf_op jit(solution)/shard_map/all_gather | solution.py:260
  203.4 116.9 %all-gather.17.cloned.1.call-start = ((), (), s32[]{:S(2)}) async-start(), calls=%async_computation.11 | async-start | bytes 1802240 | tf_op jit(solution)/shard_map/all_gather | solution.py:248
  204.0 174.6 %reduce-scatter.11.cloned.1.call-start = ((), (), s32[]{:S(2)}) async-start(), calls=%async_computation.14 | async-start | bytes 2621440 | tf_op jit(solution)/shard_map/reduce_scatter | solution.py:256
  320.3 9.5 %copy-start.178 = (bf16[1024,1408]{0,1:T(8,128)(2,1)S(1)}, bf16[1024,1408]{0,1:T(8,128)(2,1)}, u32[]{:S(2)}) copy-start(bf16[1024,1408]{0,1:T(8,128)(2,1)} %all-gather.15.cloned.1.call-done) | copy-start | bytes 8650756
  334.6 96.0 %all-gather.21.cloned.1.call-start = ((), (), s32[]{:S(2)}) async-start(), calls=%async_computation.15 | async-start | bytes 2621440 | tf_op jit(solution)/shard_map/all_gather | solution.py:260
  385.2 226.4 %reduce-scatter.13.cloned.1.call-start = ((), (), s32[]{:S(2)}) async-start(), calls=%async_computation.16 | async-start | bytes 2621440 | tf_op jit(solution)/shard_map/reduce_scatter | solution.py:256
  450.1 32.4 %collective-permute-start.2 = (bf16[2,256,128]{2,1,0:T(8,128)(2,1)}, bf16[2,256,128]{2,1,0:T(8,128)(2,1)}, u32[]{:S(2)}, u32[]{:S(2)}) collective-permute-start(bf16[2,256,128]{2,1,0:T(8,128)(2,1)} %fusion.44), channel_id=1, source_target_pairs={{4,0},{5,1},{6,2},{7,3},{12,8},{13,9},{14,10},{15,11},{20,16},{21,... | collective-permute-start | bytes 393224 | tf_op jit(solution)/shard_map/ppermute | solution.py:20
  512.6 11.2 %slice-start = ((s8[6815744]{0:T(1024)(128)(4,1)}), s8[4194304]{0:T(1024)(128)(4,1)S(1)}, s32[]{:S(2)}) async-start(s8[6815744]{0:T(1024)(128)(4,1)} %bitcast.463), calls=%async_computation.21 | async-start | bytes 8388608
  546.6 3.8 collective-permute-start.3
  559.1 8.5 copy-start.184
  567.5 89.6 %reduce-scatter.9.cloned.1.call-start = ((), (), s32[]{:S(2)}) async-start(), calls=%async_computation.12 | async-start | bytes 2621440 | tf_op jit(solution)/shard_map/reduce_scatter | solution.py:256
  572.0 133.7 %reduce-scatter.15.cloned.1.call-start = ((), (), s32[]{:S(2)}) async-start(), calls=%async_computation.18 | async-start | bytes 4259840 | tf_op jit(solution)/shard_map/reduce_scatter | solution.py:366
  581.2 191.0 %reduce-scatter.17.cloned.1.call-start = ((), (), s32[]{:S(2)}) async-start(), calls=%async_computation.19 | async-start | bytes 6881280 | tf_op jit(solution)/shard_map/reduce_scatter | solution.py:366
  607.9 49.3 %copy-start.24 = (bf16[256,1024]{1,0:T(8,128)(2,1)S(1)}, bf16[256,1024]{1,0:T(8,128)(2,1)}, u32[]{:S(2)}) copy-start(bf16[256,1024]{1,0:T(8,128)(2,1)} %reduce-scatter.7.cloned.1.call-done) | copy-start | bytes 1572868
  607.9 49.3 %copy-start.49 = (bf16[256,1024]{1,0:T(8,128)(2,1)S(1)}, bf16[256,1024]{1,0:T(8,128)(2,1)}, u32[]{:S(2)}) copy-start(bf16[256,1024]{1,0:T(8,128)(2,1)} %reduce-scatter.11.cloned.1.call-done) | copy-start | bytes 1572868
  607.9 49.2 %copy-start.115 = (f32[1024]{0:T(1024)S(1)}, f32[1024]{0:T(1024)}, u32[]{:S(2)}) copy-start(f32[1024]{0:T(1024)} %param.38) | copy-start | bytes 12292
  607.9 49.2 %copy-start.123 = (f32[256]{0:T(256)S(1)}, f32[256]{0:T(256)}, u32[]{:S(2)}) copy-start(f32[256]{0:T(256)} %copy-done.122) | copy-start | bytes 3076
  607.9 49.2 %copy-start.147 = (f32[256]{0:T(256)S(1)}, f32[256]{0:T(256)}, u32[]{:S(2)}) copy-start(f32[256]{0:T(256)} %copy-done.146) | copy-start | bytes 3076
  607.9 224.4 %all-gather.23.cloned.1.call-start = ((), (), s32[]{:S(2)}) async-start(), calls=%async_computation.17 | async-start | bytes 2621440 | tf_op jit(solution)/shard_map/all_gather | solution.py:260
  660.2 112.1 %copy-start.181 = (f32[2]{0:T(128)S(1)}, f32[2]{0:T(128)}, u32[]{:S(2)}) copy-start(f32[2]{0:T(128)} %param.34) | copy-start | bytes 28
  660.2 131.3 %copy-start.136 = (f32[1024]{0:T(1024)S(1)}, f32[1024]{0:T(1024)}, u32[]{:S(2)}) copy-start(f32[1024]{0:T(1024)} %get-tuple-element.87) | copy-start | bytes 12292
  660.2 131.3 %copy-start.167 = (f32[256]{0:T(256)S(1)}, f32[256]{0:T(256)}, u32[]{:S(2)}) copy-start(f32[256]{0:T(256)} %get-tuple-element.82) | copy-start | bytes 3076
  660.3 207.7 %all-gather.19.cloned.1.call-start = ((), (), s32[]{:S(2)}) async-start(), calls=%async_computation.13 | async-start | bytes 2621440 | tf_op jit(solution)/shard_map/all_gather | solution.py:260
  660.8 229.5 %all-reduce.58.cloned.1.call-start = ((), (), s32[]{:S(2)}) async-start(), calls=%async_computation.20 | async-start | bytes 4456448 | tf_op jit(solution)/shard_map/psum | solution.py:367
  (158 other events, 385.1 us)
Sparse Core Ops, SparseCore 0:
  11.3 48.8 all-gather.8
  62.0 26.4 all-gather.10
  154.6 43.8 reduce-scatter.6
  201.0 40.9 all-gather.14
  244.0 45.9 all-gather.12
  291.8 28.4 all-gather.16
  334.7 43.8 reduce-scatter.10
  385.3 45.2 all-gather.20
  567.6 43.9 reduce-scatter.12
  613.9 43.1 reduce-scatter.8
  660.2 45.4 reduce-scatter.14
  708.6 63.6 reduce-scatter.16
  774.4 46.7 all-gather.22
  823.2 44.7 all-gather.18
  870.2 20.1 all-reduce.57
